TPU v7x, 256 devices: a whole 4x4x8 slice. The times are simulated.
256 devices in a mesh: stripe: 32 (over z, x_lo, core), tile: 8 (over y, x_hi).
Axes of the slice: x: 4 (x_hi: 2, x_lo: 2; x = x_hi * 2 + x_lo), y: 4, z: 8, core: 2. Of those that a mesh axis runs over, the one named last changes fastest.
Arguments:
- positions: int32 [32, 24], P('stripe', 'tile'), may hold values from -64 to -64, as said below
- row_offsets: int32 [32, 24], P('stripe', 'tile'), may hold values from -64 to 64, as said below
- amplitudes: float32 [32, 24, 256, 256], P('stripe', 'tile'), may hold values from 0 to 2
- object_field: float32 [2, 8192, 1024], P(None, 'stripe', 'tile'), may hold values from -6 to 6
- probe_field: float32 [2, 256, 256], replicated, may hold values from -6 to 6
Outputs:
- object_out: float32 [2, 8192, 1024], P(None, 'stripe', 'tile')
- probe_out: float32 [2, 256, 256], replicated
Inputs may be any that keep to these rules, and one draw needn't show every extreme that they name: `positions`: in every block of 3 patterns of one stripe and one tile, the first offset is -64 and the second is 128 - 192. `row_offsets`: in every block of 3 patterns of one stripe and one tile, the first row offset is -64 and the second is 64.
All inputs are finite; a program needn't handle non-finite values.
Results may differ from a plain program's by a relative error of at most 0.0006.
The roundings to bfloat16 on the way count: a program that leaves them out, or rounds other values in their place, can miss the bound.
Values sent between devices are 32-bit elements; how exact they have to be, the bound alone decides.
No kernel may reach another device: no remote copies, remote signals or barrier semaphores. Data moves between devices by JAX's collectives and lax.ppermute only.
A program may use at most 64 MiB of HBM per device.

v0:
```python
import math
import jax
import jax.numpy as jnp
from jax import lax
from jax.sharding import PartitionSpec as P

PW = 256
HALO = 64
TILE_W = 128
PAT_DEV = 3
INNER = 2
OUTER = 2


def padded(x, sides, width):
    for axis, dim in sides:
        count, length = (lax.axis_size(axis), x.shape[dim])
        up = [(i, (i + 1) % count) for i in range(count - 1)]
        down = [(j, i) for i, j in up]
        last = lax.slice_in_dim(x, length - width, length, axis=dim)
        first = lax.slice_in_dim(x, 0, width, axis=dim)
        before = lax.ppermute(last, axis, up)
        after = lax.ppermute(first, axis, down)
        x = jnp.concatenate([before, x, after], axis=dim)
    return x


def from_behind(value, axis, steps):
    count = lax.axis_size(axis)
    first, last = (max(0, -steps), min(count, count - steps))
    return lax.ppermute(value, axis, [(source, source + steps) for source in range(first, last)])


def dft_tables():
    indices = jnp.arange(PW, dtype=jnp.int32)
    phase = indices[:, None] * indices[None, :] % PW
    angles = phase.astype(jnp.float32) * (2.0 * math.pi / PW)
    factor = 1.0 / math.sqrt(PW)
    return (
        (jnp.cos(angles) * factor).astype(jnp.bfloat16),
        (jnp.sin(angles) * factor).astype(jnp.bfloat16),
    )


def apply_left(matrix, batch):
    return jnp.einsum("kn,pnm->pkm", matrix, batch, preferred_element_type=jnp.float32)


def apply_right(batch, matrix):
    return jnp.einsum("pkn,nm->pkm", batch, matrix, preferred_element_type=jnp.float32)


def pattern_pass(windows, probe_field, measured, cosine, sine):
    win_re = windows[:, 0]
    win_im = windows[:, 1]
    probe_re = probe_field[0]
    probe_im = probe_field[1]
    exit_re = (probe_re * win_re - probe_im * win_im).astype(jnp.bfloat16)
    exit_im = (probe_re * win_im + probe_im * win_re).astype(jnp.bfloat16)
    half_re = (apply_left(cosine, exit_re) + apply_left(sine, exit_im)).astype(jnp.bfloat16)
    half_im = (apply_left(cosine, exit_im) - apply_left(sine, exit_re)).astype(jnp.bfloat16)
    spec_re = apply_right(half_re, cosine) + apply_right(half_im, sine)
    spec_im = apply_right(half_im, cosine) - apply_right(half_re, sine)
    magnitude = jnp.sqrt(spec_re * spec_re + spec_im * spec_im)
    scaling = measured / jnp.maximum(magnitude, 0.5)
    miss_re = (spec_re - scaling * spec_re).astype(jnp.bfloat16)
    miss_im = (spec_im - scaling * spec_im).astype(jnp.bfloat16)
    hb_re = (apply_left(cosine, miss_re) - apply_left(sine, miss_im)).astype(jnp.bfloat16)
    hb_im = (apply_left(cosine, miss_im) + apply_left(sine, miss_re)).astype(jnp.bfloat16)
    back_re = apply_right(hb_re, cosine) - apply_right(hb_im, sine)
    back_im = apply_right(hb_im, cosine) + apply_right(hb_re, sine)
    object_grad = jnp.stack(
        [probe_re * back_re + probe_im * back_im, probe_re * back_im - probe_im * back_re], axis=1
    )
    probe_grad = jnp.stack(
        [
            jnp.sum(win_re * back_re + win_im * back_im, axis=0),
            jnp.sum(win_re * back_im - win_im * back_re, axis=0),
        ]
    )
    illumination = jnp.sum(win_re * win_re + win_im * win_im, axis=0)
    return (object_grad, probe_grad, illumination)


def per_device(positions, row_offsets, amplitudes, object_field, probe_field):
    cosine, sine = dft_tables()
    column_starts = positions[0] + HALO
    row_starts = row_offsets[0] + HALO
    measured = amplitudes[0]
    rows_ext = PW + 2 * HALO
    columns_ext = TILE_W + 2 * HALO
    zero_index = jnp.zeros((), jnp.int32)
    current = object_field
    extended = object_field
    for outer_step in range(OUTER):
        grad_sum = jnp.zeros((2, PW, PW), jnp.float32)
        light_sum = jnp.zeros((PW, PW), jnp.float32)
        step_size = 1.0 / (
            2.0
            * PAT_DEV
            * jnp.max(probe_field[0] * probe_field[0] + probe_field[1] * probe_field[1])
            + 1e-06
        )
        for inner_step in range(INNER):
            extended = padded(current, (("stripe", 1), ("tile", 2)), HALO)
            windows = jax.vmap(
                lambda row_start, column_start: lax.dynamic_slice(
                    extended, (zero_index, row_start, column_start), (2, PW, PW)
                )
            )(row_starts, column_starts)
            object_grad, grad_sum, light_sum = pattern_pass(
                windows, probe_field, measured, cosine, sine
            )
            gradient = jnp.zeros((2, rows_ext, columns_ext), jnp.float32)
            for pattern in range(PAT_DEV):
                where = (zero_index, row_starts[pattern], column_starts[pattern])
                before = lax.dynamic_slice(gradient, where, (2, PW, PW))
                gradient = lax.dynamic_update_slice(gradient, before + object_grad[pattern], where)
            from_left = from_behind(gradient[:, :, HALO + TILE_W :], "tile", 1)
            from_right = from_behind(gradient[:, :, :HALO], "tile", -1)
            middle = gradient[:, :, HALO : HALO + TILE_W]
            middle = middle.at[:, :, :HALO].add(from_left)
            middle = middle.at[:, :, TILE_W - HALO :].add(from_right)
            from_above = from_behind(middle[:, HALO + PW :, :], "stripe", 1)
            from_below = from_behind(middle[:, :HALO, :], "stripe", -1)
            own_grad = middle[:, HALO : HALO + PW, :]
            own_grad = own_grad.at[:, :HALO, :].add(from_above)
            own_grad = own_grad.at[:, PW - HALO :, :].add(from_below)
            current = current - step_size * own_grad
        total_grad, total_light = lax.psum((grad_sum, light_sum), ("stripe", "tile"))
        probe_field = probe_field - 0.5 * total_grad / (total_light + 1.0)
    return (current, probe_field)


def solution(mesh):
    placed = (
        P("stripe", "tile"),
        P("stripe", "tile"),
        P("stripe", "tile", None, None),
        P(None, "stripe", "tile"),
        P(),
    )
    return jax.shard_map(
        per_device,
        mesh=mesh,
        in_specs=placed,
        out_specs=(P(None, "stripe", "tile"), P()),
        check_vma=False,
    )
```

profile of v0, /device:TPU:2, one launch (start us, length us, event | category | flops | bytes accessed | tf_op | source)
XLA Modules:
  0.0 924.7 jit_solution(10686164837930913628)
XLA Ops:
  8.2 1.9 collective-permute-start
  10.2 3.6 collective-permute-start.1
  21.8 4.1 collective-permute-start.2
  27.2 7.7 collective-permute-done.2
  35.0 11.0 %collective-permute-done.3 = f32[2,384,64]{2,0,1:T(2,128)S(1)} collective-permute-done((f32[2,384,64]{2,0,1:T(2,128)S(1)}, f32[2,384,64]{2,0,1:T(2,128)S(1)}, u32[]{:S(2)}, u32[]{:S(2)}) %collective-permute-start.3) | collective-permute-done | bytes 196640 | tf_op jit(solution)/shard_map/ppermute | solution.py:23
  47.2 2.6 gather_fusion
  70.4 12.6 %subtract_bitcast_fusion.3 = (f32[3,1,256,256]{3,2,0,1:T(8,128)S(1)}, f32[3,1,256,256]{3,2,0,1:T(8,128)S(1)}) fusion(f32[3,256,256]{2,1,0:T(8,128)S(1)} %convolution_add_fusion.12, f32[256,256]{1,0:T(8,128)S(1)} %get-tuple-element.251, f32[256,256]{1,0:T(8,128)S(1)} %get-tuple-element.250, f32[3,256,256]{2,1,0:T(8,128)S(1)} %fusion.160, ...), kind=kOutput, calls=%fused_computation.134 | convolution fusion | flops 103088128 | bytes 4063232 | tf_op jit(solution)/shard_map/pkn,nm->pkm/dot_general | solution.py:50
  83.0 3.0 dynamic_update_slice.48
  86.1 2.2 dynamic_update_slice.49
  88.4 2.2 dynamic_update_slice.50
  90.8 4.5 collective-permute-start.4
  96.7 7.2 collective-permute-done.4
  105.1 9.0 collective-permute-done.5
  115.9 1.9 collective-permute-start.6
  119.2 3.6 collective-permute-start.7
  122.9 1.9 collective-permute-done.7
  124.8 3.2 collective-permute-start.8
  128.0 2.5 collective-permute-start.9
  130.4 1.9 collective-permute-done.9
  132.5 5.2 collective-permute-start.10
  139.0 7.8 collective-permute-done.10
  146.8 9.7 %collective-permute-done.11 = f32[2,384,64]{2,1,0:T(8,128)S(1)} collective-permute-done((f32[2,384,64]{2,1,0:T(8,128)S(1)}, f32[2,384,64]{2,1,0:T(8,128)S(1)}, u32[]{:S(2)}, u32[]{:S(2)}) %collective-permute-start.11) | collective-permute-done | bytes 196640 | tf_op jit(solution)/shard_map/ppermute | solution.py:23
  157.5 2.6 gather_fusion.1
  180.7 2.8 add_reduce_fusion.3
  183.6 3.0 dynamic_update_slice.51
  186.7 2.2 dynamic_update_slice.52
  189.0 2.2 dynamic_update_slice.53
  191.4 5.3 collective-permute-start.12
  198.2 8.0 collective-permute-done.12
  207.2 8.2 collective-permute-done.13
  217.2 1.9 collective-permute-start.14
  219.1 3.6 collective-permute-start.15
  224.7 5.0 collective-permute-start.16
  229.7 1.9 collective-permute-start.17
  236.4 251.6 %all-reduce.7.cloned.1.call-done = (f32[2,256,256]{2,1,0:T(8,128)}, f32[256,256]{1,0:T(8,128)}) async-done(((f32[2,256,256]{2,1,0:T(8,128)}, f32[256,256]{1,0:T(8,128)}), (f32[2,256,256]{2,1,0:T(8,128)}, f32[256,256]{1,0:T(8,128)})) %all-reduce.7.cloned.1.call-update) | async-done | bytes 786448 | tf_op jit(solution)/shard_map/psum | solution.py:130
  492.2 2.6 gather_fusion.2
  517.9 4.0 dynamic_update_slice.54
  522.8 3.8 dynamic_update_slice.55
  527.4 3.8 dynamic_update_slice.56
  531.4 4.0 collective-permute-start.20
  536.9 5.4 collective-permute-done.20
  543.3 10.0 %collective-permute-done.21 = f32[2,384,64]{2,1,0:T(8,128)S(1)} collective-permute-done((f32[2,384,64]{2,1,0:T(8,128)S(1)}, f32[2,384,64]{2,1,0:T(8,128)S(1)}, u32[]{:S(2)}, u32[]{:S(2)}) %collective-permute-start.21) | collective-permute-done | bytes 196640 | tf_op jit(solution)/shard_map/ppermute | solution.py:31
  555.1 1.9 collective-permute-start.22
  558.4 3.6 collective-permute-start.23
  562.1 1.9 collective-permute-done.23
  564.1 4.6 collective-permute-start.24
  568.6 1.9 collective-permute-start.25
  570.6 1.9 collective-permute-done.25
  572.7 3.3 collective-permute-start.26
  577.2 7.7 collective-permute-done.26
  584.9 10.9 %collective-permute-done.27 = f32[2,384,64]{2,1,0:T(8,128)S(1)} collective-permute-done((f32[2,384,64]{2,1,0:T(8,128)S(1)}, f32[2,384,64]{2,1,0:T(8,128)S(1)}, u32[]{:S(2)}, u32[]{:S(2)}) %collective-permute-start.27) | collective-permute-done | bytes 196640 | tf_op jit(solution)/shard_map/ppermute | solution.py:23
  596.8 2.6 gather_fusion.3
  619.9 2.9 add_reduce_fusion.1
  622.9 3.0 dynamic_update_slice.57
  626.0 2.2 dynamic_update_slice.58
  628.3 2.2 dynamic_update_slice.59
  630.7 4.2 collective-permute-start.28
  636.3 7.9 collective-permute-done.28
  645.3 10.4 %collective-permute-done.29 = f32[2,384,64]{2,1,0:T(8,128)S(1)} collective-permute-done((f32[2,384,64]{2,1,0:T(8,128)S(1)}, f32[2,384,64]{2,1,0:T(8,128)S(1)}, u32[]{:S(2)}, u32[]{:S(2)}) %collective-permute-start.29) | collective-permute-done | bytes 196640 | tf_op jit(solution)/shard_map/ppermute | solution.py:31
  657.4 2.1 collective-permute-start.30
  660.4 3.6 collective-permute-start.31
  664.1 1.9 collective-permute-done.31
  666.7 247.8 %all-reduce.5.cloned.1.call-done = (f32[2,256,256]{2,1,0:T(8,128)}, f32[256,256]{1,0:T(8,128)}) async-done(((f32[2,256,256]{2,1,0:T(8,128)}, f32[256,256]{1,0:T(8,128)}), (f32[2,256,256]{2,1,0:T(8,128)}, f32[256,256]{1,0:T(8,128)})) %all-reduce.5.cloned.1.call-update) | async-done | bytes 786448 | tf_op jit(solution)/shard_map/psum | solution.py:130
  915.5 1.9 divide_subtract_fusion
  (224 shorter events, 130.4 us)
Async XLA Ops:
  7.2 13.9 %copy-start.6 = (f32[2,256,128]{2,1,0:T(8,128)S(1)}, f32[2,256,128]{2,1,0:T(8,128)}, u32[]{:S(2)}) copy-start(f32[2,256,128]{2,1,0:T(8,128)} %param.40) | copy-start | bytes 786436
  7.2 7.7 copy-start.16
  7.2 480.8 %all-reduce.7.cloned.1.call-start = ((), (), s32[]{:S(2)}) async-start(), calls=%async_computation.1 | async-start | bytes 1572864 | tf_op jit(solution)/shard_map/psum | solution.py:130
  8.2 12.9 %collective-permute-start = (f32[2,64,128]{2,0,1:T(2,128)S(1)}, f32[2,64,128]{2,0,1:T(2,128)S(1)}, u32[]{:S(2)}, u32[]{:S(2)}) collective-permute-start(f32[2,64,128]{2,0,1:T(2,128)S(1)} %copy.230), channel_id=1, source_target_pairs={{0,8},{8,16},{16,24},{24,32},{32,40},{40,48},{48,56},{56,64},{64,7... | collective-permute-start | bytes 196616 | tf_op jit(solution)/shard_map/ppermute | solution.py:22
  10.2 17.0 %copy-start.15 = (s32[1,3]{1,0:T(1,128)S(1)}, s32[1,3]{1,0:T(1,128)}, u32[]{:S(2)}) copy-start(s32[1,3]{1,0:T(1,128)} %param.37) | copy-start | bytes 40
  10.2 11.2 %collective-permute-start.1 = (f32[2,64,128]{2,0,1:T(2,128)S(1)}, f32[2,64,128]{2,0,1:T(2,128)S(1)}, u32[]{:S(2)}, u32[]{:S(2)}) collective-permute-start(f32[2,64,128]{2,0,1:T(2,128)S(1)} %copy.231), channel_id=1, source_target_pairs={{8,0},{16,8},{24,16},{32,24},{40,32},{48,40},{56,48},{64,56},{72,6... | collective-permute-start | bytes 196616 | tf_op jit(solution)/shard_map/ppermute | solution.py:23
  21.8 13.1 %collective-permute-start.2 = (f32[2,384,64]{2,0,1:T(2,128)S(1)}, f32[2,384,64]{2,0,1:T(2,128)S(1)}, u32[]{:S(2)}, u32[]{:S(2)}) collective-permute-start(f32[2,384,64]{2,0,1:T(2,128)S(1)} %get-tuple-element.266), channel_id=1, source_target_pairs={{0,1},{1,2},{2,3},{3,4},{4,5},{5,6},{6,7},{8,9},{9,10},{10,11},{11... | collective-permute-start | bytes 589832 | tf_op jit(solution)/shard_map/ppermute | solution.py:22
  25.9 20.1 %collective-permute-start.3 = (f32[2,384,64]{2,0,1:T(2,128)S(1)}, f32[2,384,64]{2,0,1:T(2,128)S(1)}, u32[]{:S(2)}, u32[]{:S(2)}) collective-permute-start(f32[2,384,64]{2,0,1:T(2,128)S(1)} %get-tuple-element.267), channel_id=1, source_target_pairs={{1,0},{2,1},{3,2},{4,3},{5,4},{6,5},{7,6},{9,8},{10,9},{11,10},{12... | collective-permute-start | bytes 589832 | tf_op jit(solution)/shard_map/ppermute | solution.py:23
  57.4 2.7 copy-start.11
  90.8 13.2 %collective-permute-start.4 = (f32[2,384,64]{2,1,0:T(8,128)S(1)}, f32[2,384,64]{2,1,0:T(8,128)S(1)}, u32[]{:S(2)}, u32[]{:S(2)}) collective-permute-start(f32[2,384,64]{2,1,0:T(8,128)S(1)} %get-tuple-element.247), channel_id=1, source_target_pairs={{0,1},{1,2},{2,3},{3,4},{4,5},{5,6},{6,7},{8,9},{9,10},{10,11},{11... | collective-permute-start | bytes 589832 | tf_op jit(solution)/shard_map/ppermute | solution.py:31
  95.4 18.7 %collective-permute-start.5 = (f32[2,384,64]{2,1,0:T(8,128)S(1)}, f32[2,384,64]{2,1,0:T(8,128)S(1)}, u32[]{:S(2)}, u32[]{:S(2)}) collective-permute-start(f32[2,384,64]{2,1,0:T(8,128)S(1)} %get-tuple-element.246), channel_id=1, source_target_pairs={{1,0},{2,1},{3,2},{4,3},{5,4},{6,5},{7,6},{9,8},{10,9},{11,10},{12... | collective-permute-start | bytes 589832 | tf_op jit(solution)/shard_map/ppermute | solution.py:31
  104.1 13.6 %copy-start.4 = (f32[2,256,256]{2,1,0:T(8,128)S(1)}, f32[2,256,256]{2,1,0:T(8,128)}, u32[]{:S(2)}) copy-start(f32[2,256,256]{2,1,0:T(8,128)} %param.41) | copy-start | bytes 1572868
  105.1 19.7 %copy-start.7 = (f32[2,256,128]{2,1,0:T(8,128)S(1)}, f32[2,256,128]{2,1,0:T(8,128)}, u32[]{:S(2)}) copy-start(f32[2,256,128]{2,1,0:T(8,128)} %param.40) | copy-start | bytes 786436
  115.9 7.0 collective-permute-start.6
  119.2 5.5 collective-permute-start.7
  124.8 5.6 collective-permute-start.8
  128.0 4.3 collective-permute-start.9
  132.5 14.3 %collective-permute-start.10 = (f32[2,384,64]{2,1,0:T(8,128)S(1)}, f32[2,384,64]{2,1,0:T(8,128)S(1)}, u32[]{:S(2)}, u32[]{:S(2)}) collective-permute-start(f32[2,384,64]{2,1,0:T(8,128)S(1)} %get-tuple-element.262), channel_id=1, source_target_pairs={{0,1},{1,2},{2,3},{3,4},{4,5},{5,6},{6,7},{8,9},{9,10},{10,11},{11... | collective-permute-start | bytes 589832 | tf_op jit(solution)/shard_map/ppermute | solution.py:22
  137.7 18.8 %collective-permute-start.11 = (f32[2,384,64]{2,1,0:T(8,128)S(1)}, f32[2,384,64]{2,1,0:T(8,128)S(1)}, u32[]{:S(2)}, u32[]{:S(2)}) collective-permute-start(f32[2,384,64]{2,1,0:T(8,128)S(1)} %get-tuple-element.263), channel_id=1, source_target_pairs={{1,0},{2,1},{3,2},{4,3},{5,4},{6,5},{7,6},{9,8},{10,9},{11,10},{12... | collective-permute-start | bytes 589832 | tf_op jit(solution)/shard_map/ppermute | solution.py:23
  167.7 2.9 copy-start.12
  191.4 14.8 %collective-permute-start.12 = (f32[2,384,64]{2,1,0:T(8,128)S(1)}, f32[2,384,64]{2,1,0:T(8,128)S(1)}, u32[]{:S(2)}, u32[]{:S(2)}) collective-permute-start(f32[2,384,64]{2,1,0:T(8,128)S(1)} %get-tuple-element.245), channel_id=1, source_target_pairs={{0,1},{1,2},{2,3},{3,4},{4,5},{5,6},{6,7},{8,9},{9,10},{10,11},{11... | collective-permute-start | bytes 589832 | tf_op jit(solution)/shard_map/ppermute | solution.py:31
  196.9 18.5 %collective-permute-start.13 = (f32[2,384,64]{2,1,0:T(8,128)S(1)}, f32[2,384,64]{2,1,0:T(8,128)S(1)}, u32[]{:S(2)}, u32[]{:S(2)}) collective-permute-start(f32[2,384,64]{2,1,0:T(8,128)S(1)} %get-tuple-element.244), channel_id=1, source_target_pairs={{1,0},{2,1},{3,2},{4,3},{5,4},{6,5},{7,6},{9,8},{10,9},{11,10},{12... | collective-permute-start | bytes 589832 | tf_op jit(solution)/shard_map/ppermute | solution.py:31
  215.6 16.1 %copy-start.8 = (f32[256,256]{1,0:T(8,128)S(1)}, f32[256,256]{1,0:T(8,128)}, u32[]{:S(2)}) copy-start(f32[256,256]{1,0:T(8,128)} %get-tuple-element.197) | copy-start | bytes 786436
  217.2 5.6 collective-permute-start.14
  219.1 5.5 collective-permute-start.15
  224.7 265.5 %copy-start = (f32[2,256,128]{2,1,0:T(8,128)}, f32[2,256,128]{2,1,0:T(8,128)S(1)}, u32[]{:S(2)}) copy-start(f32[2,256,128]{2,1,0:T(8,128)S(1)} %multiply_subtract_fusion.10) | copy-start | bytes 786436
  224.7 7.8 collective-permute-start.16
  229.7 3.8 collective-permute-start.17
  232.5 256.5 %copy-start.5 = (f32[2,256,256]{2,1,0:T(8,128)S(1)}, f32[2,256,256]{2,1,0:T(8,128)}, u32[]{:S(2)}) copy-start(f32[2,256,256]{2,1,0:T(8,128)} %param.41) | copy-start | bytes 1572868
  232.5 682.0 %all-reduce.5.cloned.1.call-start = ((), (), s32[]{:S(2)}) async-start(), calls=%async_computation | async-start | bytes 1572864 | tf_op jit(solution)/shard_map/psum | solution.py:130
  233.7 256.4 %collective-permute-start.18 = (f32[2,384,64]{2,1,0:T(8,128)S(1)}, f32[2,384,64]{2,1,0:T(8,128)S(1)}, u32[]{:S(2)}, u32[]{:S(2)}) collective-permute-start(f32[2,384,64]{2,1,0:T(8,128)S(1)} %get-tuple-element.258), channel_id=1, source_target_pairs={{0,1},{1,2},{2,3},{3,4},{4,5},{5,6},{6,7},{8,9},{9,10},{10,11},{11... | collective-permute-start | bytes 589832 | tf_op jit(solution)/shard_map/ppermute | solution.py:22
  235.1 255.1 %collective-permute-start.19 = (f32[2,384,64]{2,1,0:T(8,128)S(1)}, f32[2,384,64]{2,1,0:T(8,128)}, u32[]{:S(2)}, u32[]{:S(2)}) collective-permute-start(f32[2,384,64]{2,1,0:T(8,128)S(1)} %get-tuple-element.259), channel_id=1, source_target_pairs={{1,0},{2,1},{3,2},{4,3},{5,4},{6,5},{7,6},{9,8},{10,9},{11,10},{12... | collective-permute-start | bytes 589832 | tf_op jit(solution)/shard_map/ppermute | solution.py:23
  502.4 2.9 copy-start.13
  531.4 10.8 %collective-permute-start.20 = (f32[2,384,64]{2,1,0:T(8,128)S(1)}, f32[2,384,64]{2,1,0:T(8,128)S(1)}, u32[]{:S(2)}, u32[]{:S(2)}) collective-permute-start(f32[2,384,64]{2,1,0:T(8,128)S(1)} %get-tuple-element.243), channel_id=1, source_target_pairs={{0,1},{1,2},{2,3},{3,4},{4,5},{5,6},{6,7},{8,9},{9,10},{10,11},{11... | collective-permute-start | bytes 589832 | tf_op jit(solution)/shard_map/ppermute | solution.py:31
  535.6 17.8 %collective-permute-start.21 = (f32[2,384,64]{2,1,0:T(8,128)S(1)}, f32[2,384,64]{2,1,0:T(8,128)S(1)}, u32[]{:S(2)}, u32[]{:S(2)}) collective-permute-start(f32[2,384,64]{2,1,0:T(8,128)S(1)} %get-tuple-element.242), channel_id=1, source_target_pairs={{1,0},{2,1},{3,2},{4,3},{5,4},{6,5},{7,6},{9,8},{10,9},{11,10},{12... | collective-permute-start | bytes 589832 | tf_op jit(solution)/shard_map/ppermute | solution.py:31
  543.3 20.6 %copy-start.1 = (f32[2,256,128]{2,1,0:T(8,128)S(1)}, f32[2,256,128]{2,1,0:T(8,128)}, u32[]{:S(2)}) copy-start(f32[2,256,128]{2,1,0:T(8,128)} %copy-done) | copy-start | bytes 786436
  555.1 7.0 collective-permute-start.22
  558.4 5.5 collective-permute-start.23
  564.0 31.8 %copy-start.2 = (f32[2,256,128]{2,1,0:T(8,128)}, f32[2,256,128]{2,1,0:T(8,128)S(1)}, u32[]{:S(2)}) copy-start(f32[2,256,128]{2,1,0:T(8,128)S(1)} %multiply_subtract_fusion.9) | copy-start | bytes 786436
  564.1 6.5 collective-permute-start.24
  568.6 3.8 collective-permute-start.25
  572.7 12.3 %collective-permute-start.26 = (f32[2,384,64]{2,1,0:T(8,128)S(1)}, f32[2,384,64]{2,1,0:T(8,128)S(1)}, u32[]{:S(2)}, u32[]{:S(2)}) collective-permute-start(f32[2,384,64]{2,1,0:T(8,128)S(1)} %get-tuple-element.254), channel_id=1, source_target_pairs={{0,1},{1,2},{2,3},{3,4},{4,5},{5,6},{6,7},{8,9},{9,10},{10,11},{11... | collective-permute-start | bytes 589832 | tf_op jit(solution)/shard_map/ppermute | solution.py:22
  575.9 19.9 %collective-permute-start.27 = (f32[2,384,64]{2,1,0:T(8,128)S(1)}, f32[2,384,64]{2,1,0:T(8,128)S(1)}, u32[]{:S(2)}, u32[]{:S(2)}) collective-permute-start(f32[2,384,64]{2,1,0:T(8,128)S(1)} %get-tuple-element.255), channel_id=1, source_target_pairs={{1,0},{2,1},{3,2},{4,3},{5,4},{6,5},{7,6},{9,8},{10,9},{11,10},{12... | collective-permute-start | bytes 589832 | tf_op jit(solution)/shard_map/ppermute | solution.py:23
  607.0 2.7 copy-start.14
  630.7 13.5 %collective-permute-start.28 = (f32[2,384,64]{2,1,0:T(8,128)S(1)}, f32[2,384,64]{2,1,0:T(8,128)S(1)}, u32[]{:S(2)}, u32[]{:S(2)}) collective-permute-start(f32[2,384,64]{2,1,0:T(8,128)S(1)} %get-tuple-element.241), channel_id=1, source_target_pairs={{0,1},{1,2},{2,3},{3,4},{4,5},{5,6},{6,7},{8,9},{9,10},{10,11},{11... | collective-permute-start | bytes 589832 | tf_op jit(solution)/shard_map/ppermute | solution.py:31
  635.0 20.6 %collective-permute-start.29 = (f32[2,384,64]{2,1,0:T(8,128)S(1)}, f32[2,384,64]{2,1,0:T(8,128)S(1)}, u32[]{:S(2)}, u32[]{:S(2)}) collective-permute-start(f32[2,384,64]{2,1,0:T(8,128)S(1)} %get-tuple-element.240), channel_id=1, source_target_pairs={{1,0},{2,1},{3,2},{4,3},{5,4},{6,5},{7,6},{9,8},{10,9},{11,10},{12... | collective-permute-start | bytes 589832 | tf_op jit(solution)/shard_map/ppermute | solution.py:31
  644.4 15.1 %copy-start.9 = (f32[256,256]{1,0:T(8,128)S(1)}, f32[256,256]{1,0:T(8,128)}, u32[]{:S(2)}) copy-start(f32[256,256]{1,0:T(8,128)} %get-tuple-element.194) | copy-start | bytes 786436
  644.4 15.1 %copy-start.10 = (f32[256,256]{1,0:T(8,128)S(1)}, f32[256,256]{1,0:T(8,128)}, u32[]{:S(2)}) copy-start(f32[256,256]{1,0:T(8,128)} %get-tuple-element.195) | copy-start | bytes 786436
  657.4 8.5 copy-start.3
  657.4 6.6 collective-permute-start.30
  660.4 5.5 collective-permute-start.31
Sparse Core Ops, SparseCore 0:
  232.6 255.3 all-reduce.6
  660.5 253.9 all-reduce.4
where the time goes:
time: 935 us; the launch traced here: 925 us
  waiting for transfers between devices  632 us (68%)
  matrix products  95.6 us (10%)
  starting transfers between devices  89.1 us (10%)
  local copies, waits for them, and re-layouts  66.5 us (7%)
  between operations  23.1 us (2%)
  other arithmetic  18 us (2%)
    psum x2, waiting for transfers between devices, per_device(): lax.psum((grad_sum, light_sum), ('stripe', 'tile'))  499 us
    ppermute x16, waiting for transfers between devices, from_behind(): lax.ppermute(value, axis, [(source, source + steps) for source in range(f...  73.4 us
    dot_general x32, matrix products, apply_right(): jnp.einsum('pkn,nm->pkm', batch, matrix, preferred_element_type=jnp.float32)  56.7 us
    ppermute x16, starting transfers between devices, from_behind(): lax.ppermute(value, axis, [(source, source + steps) for source in range(f...  45.5 us
    dot_general x32, matrix products, apply_left(): jnp.einsum('kn,pnm->pkm', matrix, batch, preferred_element_type=jnp.float32)  38.9 us
    ppermute x8, waiting for transfers between devices, padded(): after = lax.ppermute(first, axis, down)  36.3 us
    dynamic_update_slice x12, local copies, waits for them, and re-layouts, per_device(): lax.dynamic_update_slice(gradient, before + object_grad[pattern], where)  33.7 us
    ppermute x8, starting transfers between devices, padded(): before = lax.ppermute(last, axis, up)  28.4 us
  transfers between devices with their start and end apart: 34, of which 23 were waited for; matrix products, arithmetic and copies ran while one was open for 1% of the time, Pallas kernels for 0%

commit v1 on v0

--- a/solution.py
+++ b/solution.py
@@ -10,6 +10,12 @@
 PAT_DEV = 3
 INNER = 2
 OUTER = 2
+
+
+def make_the_notes(z_in, which_axis, net_axis):
+    for idx in (which_axis, net_axis):
+        z_in = lax.psum(z_in, idx)
+    return z_in
 
 
 def padded(x, sides, width):
@@ -127,7 +133,7 @@
             own_grad = own_grad.at[:, :HALO, :].add(from_above)
             own_grad = own_grad.at[:, PW - HALO :, :].add(from_below)
             current = current - step_size * own_grad
-        total_grad, total_light = lax.psum((grad_sum, light_sum), ("stripe", "tile"))
+        total_grad, total_light = make_the_notes((grad_sum, light_sum), "stripe", "tile")
         probe_field = probe_field - 0.5 * total_grad / (total_light + 1.0)
     return (current, probe_field)
 

time: 935 us -> 1030 us (1.10)
  waiting for transfers between devices: 632 us -> 717 us
    psum x2 -> x4, waiting for transfers between devices: 499 us -> 564 us  [make_the_notes(): z_in = lax.psum(z_in, idx)]
    ppermute x8, waiting for transfers between devices: 36.3 us -> 51.3 us  [padded(): after = lax.ppermute(first, axis, down)]
  transfers between devices with their start and end apart: 34 -> 36, of which waited for: 23 -> 27; matrix products, arithmetic and copies ran while one was open for 1% -> 2% of each run, Pallas kernels for 0% -> 0%
where the time goes in v1:
time: 1030 us; the launch traced here: 1010 us
  waiting for transfers between devices  717 us (70%)
  matrix products  95.6 us (9%)
  starting transfers between devices  92.6 us (9%)
  local copies, waits for them, and re-layouts  67.9 us (7%)
  between operations  23.1 us (2%)
  other arithmetic  18.1 us (2%)
    psum x4, waiting for transfers between devices, make_the_notes(): z_in = lax.psum(z_in, idx)  564 us
    ppermute x16, waiting for transfers between devices, from_behind(): lax.ppermute(value, axis, [(source, source + steps) for source in range(f...  72.9 us
    dot_general x32, matrix products, apply_right(): jnp.einsum('pkn,nm->pkm', batch, matrix, preferred_element_type=jnp.float32)  56.8 us
    ppermute x8, waiting for transfers between devices, padded(): after = lax.ppermute(first, axis, down)  51.3 us
    ppermute x16, starting transfers between devices, from_behind(): lax.ppermute(value, axis, [(source, source + steps) for source in range(f...  45.7 us
    dot_general x32, matrix products, apply_left(): jnp.einsum('kn,pnm->pkm', matrix, batch, preferred_element_type=jnp.float32)  38.9 us
    dynamic_update_slice x12, local copies, waits for them, and re-layouts, per_device(): lax.dynamic_update_slice(gradient, before + object_grad[pattern], where)  33.7 us
    ppermute x8, starting transfers between devices, padded(): before = lax.ppermute(last, axis, up)  31.7 us
  transfers between devices with their start and end apart: 36, of which 27 were waited for; matrix products, arithmetic and copies ran while one was open for 2% of the time, Pallas kernels for 0%

profile of v1, /device:TPU:2, one launch (start us, length us, event | category | flops | bytes accessed | tf_op | source)
XLA Modules:
  0.0 1014.9 jit_solution(14021291951107539343)
XLA Ops:
  8.2 1.9 collective-permute-start
  10.2 3.6 collective-permute-start.1
  22.3 4.1 collective-permute-start.2
  27.7 7.7 collective-permute-done.2
  35.4 11.0 %collective-permute-done.3 = f32[2,384,64]{2,0,1:T(2,128)S(1)} collective-permute-done((f32[2,384,64]{2,0,1:T(2,128)S(1)}, f32[2,384,64]{2,0,1:T(2,128)S(1)}, u32[]{:S(2)}, u32[]{:S(2)}) %collective-permute-start.3) | collective-permute-done | bytes 196640 | tf_op jit(solution)/shard_map/ppermute | solution.py:29
  47.7 2.6 gather_fusion
  70.8 12.6 %subtract_bitcast_fusion.3 = (f32[3,1,256,256]{3,2,0,1:T(8,128)S(1)}, f32[3,1,256,256]{3,2,0,1:T(8,128)S(1)}) fusion(f32[3,256,256]{2,1,0:T(8,128)S(1)} %convolution_add_fusion.12, f32[256,256]{1,0:T(8,128)S(1)} %get-tuple-element.255, f32[256,256]{1,0:T(8,128)S(1)} %get-tuple-element.254, f32[3,256,256]{2,1,0:T(8,128)S(1)} %fusion.160, ...), kind=kOutput, calls=%fused_computation.134 | convolution fusion | flops 103088128 | bytes 4063232 | tf_op jit(solution)/shard_map/pkn,nm->pkm/dot_general | solution.py:56
  83.5 3.0 dynamic_update_slice.48
  86.5 2.2 dynamic_update_slice.49
  88.8 2.2 dynamic_update_slice.50
  91.2 4.5 collective-permute-start.4
  97.2 7.2 collective-permute-done.4
  105.5 9.0 collective-permute-done.5
  116.3 1.9 collective-permute-start.6
  119.6 3.6 collective-permute-start.7
  125.2 3.2 collective-permute-start.8
  128.4 2.5 collective-permute-start.9
  133.0 5.2 collective-permute-start.10
  139.4 7.8 collective-permute-done.10
  147.3 9.7 collective-permute-done.11
  157.9 2.6 gather_fusion.1
  181.2 2.8 add_reduce_fusion.3
  184.0 3.0 dynamic_update_slice.51
  187.1 2.2 dynamic_update_slice.52
  189.4 2.2 dynamic_update_slice.53
  191.8 5.3 collective-permute-start.12
  198.6 8.0 collective-permute-done.12
  207.7 8.1 collective-permute-done.13
  217.6 1.9 collective-permute-start.14
  220.4 3.6 collective-permute-start.15
  226.1 5.0 collective-permute-start.16
  231.1 1.9 collective-permute-start.17
  234.9 209.2 %all-reduce.11.cloned.1.call-done = (f32[2,256,256]{2,1,0:T(8,128)}, f32[256,256]{1,0:T(8,128)}) async-done(((f32[2,256,256]{2,1,0:T(8,128)}, f32[256,256]{1,0:T(8,128)}), (f32[2,256,256]{2,1,0:T(8,128)}, f32[256,256]{1,0:T(8,128)})) %all-reduce.11.cloned.1.call-update) | async-done | bytes 786448 | tf_op jit(solution)/shard_map/psum | solution.py:17
  444.4 4.0 collective-permute-start.18
  449.7 7.4 collective-permute-done.18
  457.0 14.7 %collective-permute-done.19 = f32[2,384,64]{2,1,0:T(8,128)S(1)} collective-permute-done((f32[2,384,64]{2,1,0:T(8,128)S(1)}, f32[2,384,64]{2,1,0:T(8,128)S(1)}, u32[]{:S(2)}, u32[]{:S(2)}) %collective-permute-start.19) | collective-permute-done | bytes 196640 | tf_op jit(solution)/shard_map/ppermute | solution.py:29
  472.7 2.6 gather_fusion.2
  475.3 2.4 fusion.503
  477.7 66.3 %all-reduce.15.cloned.1.call-done = (f32[2,256,256]{2,1,0:T(8,128)}, f32[256,256]{1,0:T(8,128)}) async-done(((f32[2,256,256]{2,1,0:T(8,128)}, f32[256,256]{1,0:T(8,128)}), (f32[2,256,256]{2,1,0:T(8,128)}, f32[256,256]{1,0:T(8,128)})) %all-reduce.15.cloned.1.call-update) | async-done | bytes 786448 | tf_op jit(solution)/shard_map/psum | solution.py:17
  568.3 4.0 dynamic_update_slice.54
  573.2 3.8 dynamic_update_slice.55
  577.9 3.8 dynamic_update_slice.56
  581.8 2.0 collective-permute-start.20
  585.3 3.8 collective-permute-done.20
  590.2 9.1 collective-permute-done.21
  601.1 1.9 collective-permute-start.22
  604.4 3.6 collective-permute-start.23
  610.1 5.1 collective-permute-start.24
  615.2 1.9 collective-permute-start.25
  619.2 3.3 collective-permute-start.26
  623.8 6.4 collective-permute-done.26
  630.2 10.4 %collective-permute-done.27 = f32[2,384,64]{2,1,0:T(8,128)S(1)} collective-permute-done((f32[2,384,64]{2,1,0:T(8,128)S(1)}, f32[2,384,64]{2,1,0:T(8,128)S(1)}, u32[]{:S(2)}, u32[]{:S(2)}) %collective-permute-start.27) | collective-permute-done | bytes 196640 | tf_op jit(solution)/shard_map/ppermute | solution.py:29
  641.6 2.6 gather_fusion.3
  664.7 3.0 add_reduce_fusion.1
  667.8 3.0 dynamic_update_slice.57
  670.8 2.2 dynamic_update_slice.58
  673.1 2.2 dynamic_update_slice.59
  677.4 4.8 collective-permute-start.28
  683.7 6.9 collective-permute-done.28
  691.7 13.2 %collective-permute-done.29 = f32[2,384,64]{2,1,0:T(8,128)S(1)} collective-permute-done((f32[2,384,64]{2,1,0:T(8,128)S(1)}, f32[2,384,64]{2,1,0:T(8,128)S(1)}, u32[]{:S(2)}, u32[]{:S(2)}) %collective-permute-start.29) | collective-permute-done | bytes 196640 | tf_op jit(solution)/shard_map/ppermute | solution.py:37
  706.7 199.1 %all-reduce.9.cloned.1.call-done = (f32[2,256,256]{2,1,0:T(8,128)}, f32[256,256]{1,0:T(8,128)}) async-done(((f32[2,256,256]{2,1,0:T(8,128)}, f32[256,256]{1,0:T(8,128)}), (f32[2,256,256]{2,1,0:T(8,128)}, f32[256,256]{1,0:T(8,128)})) %all-reduce.9.cloned.1.call-update) | async-done | bytes 786448 | tf_op jit(solution)/shard_map/psum | solution.py:17
  905.8 2.1 collective-permute-start.30
  907.9 5.2 collective-permute-start.31
  915.8 89.3 %all-reduce.13.cloned.1.call-done = (f32[2,256,256]{2,1,0:T(8,128)}, f32[256,256]{1,0:T(8,128)}) async-done(((f32[2,256,256]{2,1,0:T(8,128)}, f32[256,256]{1,0:T(8,128)}), (f32[2,256,256]{2,1,0:T(8,128)}, f32[256,256]{1,0:T(8,128)})) %all-reduce.13.cloned.1.call-update) | async-done | bytes 786448 | tf_op jit(solution)/shard_map/psum | solution.py:17
  (230 shorter events, 140.5 us)
Async XLA Ops:
  7.2 14.4 %copy-start.8 = (f32[2,256,128]{2,1,0:T(8,128)S(1)}, f32[2,256,128]{2,1,0:T(8,128)}, u32[]{:S(2)}) copy-start(f32[2,256,128]{2,1,0:T(8,128)} %param.40) | copy-start | bytes 786436
  7.2 7.7 copy-start.16
  7.2 436.9 %all-reduce.11.cloned.1.call-start = ((), (), s32[]{:S(2)}) async-start(), calls=%async_computation.1 | async-start | bytes 1572864 | tf_op jit(solution)/shard_map/psum | solution.py:17
  8.2 13.3 %collective-permute-start = (f32[2,64,128]{2,0,1:T(2,128)S(1)}, f32[2,64,128]{2,0,1:T(2,128)S(1)}, u32[]{:S(2)}, u32[]{:S(2)}) collective-permute-start(f32[2,64,128]{2,0,1:T(2,128)S(1)} %copy.230), channel_id=1, source_target_pairs={{0,8},{8,16},{16,24},{24,32},{32,40},{40,48},{48,56},{56,64},{64,7... | collective-permute-start | bytes 196616 | tf_op jit(solution)/shard_map/ppermute | solution.py:28
  10.2 17.5 %copy-start.15 = (s32[1,3]{1,0:T(1,128)S(1)}, s32[1,3]{1,0:T(1,128)}, u32[]{:S(2)}) copy-start(s32[1,3]{1,0:T(1,128)} %param.37) | copy-start | bytes 40
  10.2 11.6 %collective-permute-start.1 = (f32[2,64,128]{2,0,1:T(2,128)S(1)}, f32[2,64,128]{2,0,1:T(2,128)S(1)}, u32[]{:S(2)}, u32[]{:S(2)}) collective-permute-start(f32[2,64,128]{2,0,1:T(2,128)S(1)} %copy.231), channel_id=1, source_target_pairs={{8,0},{16,8},{24,16},{32,24},{40,32},{48,40},{56,48},{64,56},{72,6... | collective-permute-start | bytes 196616 | tf_op jit(solution)/shard_map/ppermute | solution.py:29
  22.3 13.1 %collective-permute-start.2 = (f32[2,384,64]{2,0,1:T(2,128)S(1)}, f32[2,384,64]{2,0,1:T(2,128)S(1)}, u32[]{:S(2)}, u32[]{:S(2)}) collective-permute-start(f32[2,384,64]{2,0,1:T(2,128)S(1)} %get-tuple-element.270), channel_id=1, source_target_pairs={{0,1},{1,2},{2,3},{3,4},{4,5},{5,6},{6,7},{8,9},{9,10},{10,11},{11... | collective-permute-start | bytes 589832 | tf_op jit(solution)/shard_map/ppermute | solution.py:28
  26.3 20.1 %collective-permute-start.3 = (f32[2,384,64]{2,0,1:T(2,128)S(1)}, f32[2,384,64]{2,0,1:T(2,128)S(1)}, u32[]{:S(2)}, u32[]{:S(2)}) collective-permute-start(f32[2,384,64]{2,0,1:T(2,128)S(1)} %get-tuple-element.271), channel_id=1, source_target_pairs={{1,0},{2,1},{3,2},{4,3},{5,4},{6,5},{7,6},{9,8},{10,9},{11,10},{12... | collective-permute-start | bytes 589832 | tf_op jit(solution)/shard_map/ppermute | solution.py:29
  57.9 2.7 copy-start.11
  91.2 13.2 %collective-permute-start.4 = (f32[2,384,64]{2,1,0:T(8,128)S(1)}, f32[2,384,64]{2,1,0:T(8,128)S(1)}, u32[]{:S(2)}, u32[]{:S(2)}) collective-permute-start(f32[2,384,64]{2,1,0:T(8,128)S(1)} %get-tuple-element.251), channel_id=1, source_target_pairs={{0,1},{1,2},{2,3},{3,4},{4,5},{5,6},{6,7},{8,9},{9,10},{10,11},{11... | collective-permute-start | bytes 589832 | tf_op jit(solution)/shard_map/ppermute | solution.py:37
  95.9 18.7 %collective-permute-start.5 = (f32[2,384,64]{2,1,0:T(8,128)S(1)}, f32[2,384,64]{2,1,0:T(8,128)S(1)}, u32[]{:S(2)}, u32[]{:S(2)}) collective-permute-start(f32[2,384,64]{2,1,0:T(8,128)S(1)} %get-tuple-element.250), channel_id=1, source_target_pairs={{1,0},{2,1},{3,2},{4,3},{5,4},{6,5},{7,6},{9,8},{10,9},{11,10},{12... | collective-permute-start | bytes 589832 | tf_op jit(solution)/shard_map/ppermute | solution.py:37
  104.6 13.6 %copy-start.4 = (f32[2,256,256]{2,1,0:T(8,128)S(1)}, f32[2,256,256]{2,1,0:T(8,128)}, u32[]{:S(2)}) copy-start(f32[2,256,256]{2,1,0:T(8,128)} %param.41) | copy-start | bytes 1572868
  105.5 19.7 %copy-start.9 = (f32[2,256,128]{2,1,0:T(8,128)S(1)}, f32[2,256,128]{2,1,0:T(8,128)}, u32[]{:S(2)}) copy-start(f32[2,256,128]{2,1,0:T(8,128)} %param.40) | copy-start | bytes 786436
  116.3 7.0 collective-permute-start.6
  119.6 5.5 collective-permute-start.7
  125.2 5.6 collective-permute-start.8
  128.4 4.3 collective-permute-start.9
  133.0 14.3 %collective-permute-start.10 = (f32[2,384,64]{2,1,0:T(8,128)S(1)}, f32[2,384,64]{2,1,0:T(8,128)S(1)}, u32[]{:S(2)}, u32[]{:S(2)}) collective-permute-start(f32[2,384,64]{2,1,0:T(8,128)S(1)} %get-tuple-element.266), channel_id=1, source_target_pairs={{0,1},{1,2},{2,3},{3,4},{4,5},{5,6},{6,7},{8,9},{9,10},{10,11},{11... | collective-permute-start | bytes 589832 | tf_op jit(solution)/shard_map/ppermute | solution.py:28
  138.1 18.8 %collective-permute-start.11 = (f32[2,384,64]{2,1,0:T(8,128)S(1)}, f32[2,384,64]{2,1,0:T(8,128)S(1)}, u32[]{:S(2)}, u32[]{:S(2)}) collective-permute-start(f32[2,384,64]{2,1,0:T(8,128)S(1)} %get-tuple-element.267), channel_id=1, source_target_pairs={{1,0},{2,1},{3,2},{4,3},{5,4},{6,5},{7,6},{9,8},{10,9},{11,10},{12... | collective-permute-start | bytes 589832 | tf_op jit(solution)/shard_map/ppermute | solution.py:29
  168.1 2.9 copy-start.12
  191.8 14.8 %collective-permute-start.12 = (f32[2,384,64]{2,1,0:T(8,128)S(1)}, f32[2,384,64]{2,1,0:T(8,128)S(1)}, u32[]{:S(2)}, u32[]{:S(2)}) collective-permute-start(f32[2,384,64]{2,1,0:T(8,128)S(1)} %get-tuple-element.249), channel_id=1, source_target_pairs={{0,1},{1,2},{2,3},{3,4},{4,5},{5,6},{6,7},{8,9},{9,10},{10,11},{11... | collective-permute-start | bytes 589832 | tf_op jit(solution)/shard_map/ppermute | solution.py:37
  197.3 18.5 %collective-permute-start.13 = (f32[2,384,64]{2,1,0:T(8,128)S(1)}, f32[2,384,64]{2,1,0:T(8,128)S(1)}, u32[]{:S(2)}, u32[]{:S(2)}) collective-permute-start(f32[2,384,64]{2,1,0:T(8,128)S(1)} %get-tuple-element.248), channel_id=1, source_target_pairs={{1,0},{2,1},{3,2},{4,3},{5,4},{6,5},{7,6},{9,8},{10,9},{11,10},{12... | collective-permute-start | bytes 589832 | tf_op jit(solution)/shard_map/ppermute | solution.py:37
  206.7 12.8 %copy-start.10 = (f32[256,256]{1,0:T(8,128)S(1)}, f32[256,256]{1,0:T(8,128)}, u32[]{:S(2)}) copy-start(f32[256,256]{1,0:T(8,128)} %get-tuple-element.197) | copy-start | bytes 786436
  217.6 6.5 collective-permute-start.14
  220.4 323.6 %all-reduce.15.cloned.1.call-start = ((), (), s32[]{:S(2)}) async-start(), calls=%async_computation.3 | async-start | bytes 1572864 | tf_op jit(solution)/shard_map/psum | solution.py:17
  220.4 5.5 collective-permute-start.15
  226.0 245.7 %copy-start = (f32[2,256,128]{2,1,0:T(8,128)}, f32[2,256,128]{2,1,0:T(8,128)S(1)}, u32[]{:S(2)}) copy-start(f32[2,256,128]{2,1,0:T(8,128)S(1)} %multiply_subtract_fusion.10) | copy-start | bytes 786436
  226.1 6.9 collective-permute-start.16
  231.1 3.8 collective-permute-start.17
  444.1 461.6 %all-reduce.9.cloned.1.call-start = ((), (), s32[]{:S(2)}) async-start(), calls=%async_computation | async-start | bytes 1572864 | tf_op jit(solution)/shard_map/psum | solution.py:17
  444.4 12.7 %collective-permute-start.18 = (f32[2,384,64]{2,1,0:T(8,128)S(1)}, f32[2,384,64]{2,1,0:T(8,128)S(1)}, u32[]{:S(2)}, u32[]{:S(2)}) collective-permute-start(f32[2,384,64]{2,1,0:T(8,128)S(1)} %get-tuple-element.262), channel_id=1, source_target_pairs={{0,1},{1,2},{2,3},{3,4},{4,5},{5,6},{6,7},{8,9},{9,10},{10,11},{11... | collective-permute-start | bytes 589832 | tf_op jit(solution)/shard_map/ppermute | solution.py:28
  448.4 23.3 %collective-permute-start.19 = (f32[2,384,64]{2,1,0:T(8,128)S(1)}, f32[2,384,64]{2,1,0:T(8,128)S(1)}, u32[]{:S(2)}, u32[]{:S(2)}) collective-permute-start(f32[2,384,64]{2,1,0:T(8,128)S(1)} %get-tuple-element.263), channel_id=1, source_target_pairs={{1,0},{2,1},{3,2},{4,3},{5,4},{6,5},{7,6},{9,8},{10,9},{11,10},{12... | collective-permute-start | bytes 589832 | tf_op jit(solution)/shard_map/ppermute | solution.py:29
  475.3 69.7 %copy-start.5 = (f32[2,256,256]{2,1,0:T(8,128)S(1)}, f32[2,256,256]{2,1,0:T(8,128)}, u32[]{:S(2)}) copy-start(f32[2,256,256]{2,1,0:T(8,128)} %param.41) | copy-start | bytes 1572868
  545.0 1.3 copy-start.6
  545.0 1.5 copy-start.7
  552.8 2.9 copy-start.13
  581.8 7.3 collective-permute-start.20
  584.0 15.3 %collective-permute-start.21 = (f32[2,384,64]{2,1,0:T(8,128)S(1)}, f32[2,384,64]{2,1,0:T(8,128)S(1)}, u32[]{:S(2)}, u32[]{:S(2)}) collective-permute-start(f32[2,384,64]{2,1,0:T(8,128)S(1)} %get-tuple-element.246), channel_id=1, source_target_pairs={{1,0},{2,1},{3,2},{4,3},{5,4},{6,5},{7,6},{9,8},{10,9},{11,10},{12... | collective-permute-start | bytes 589832 | tf_op jit(solution)/shard_map/ppermute | solution.py:37
  590.2 19.8 %copy-start.1 = (f32[2,256,128]{2,1,0:T(8,128)S(1)}, f32[2,256,128]{2,1,0:T(8,128)}, u32[]{:S(2)}) copy-start(f32[2,256,128]{2,1,0:T(8,128)} %copy-done) | copy-start | bytes 786436
  601.1 7.0 collective-permute-start.22
  604.4 5.5 collective-permute-start.23
  610.0 30.6 %copy-start.2 = (f32[2,256,128]{2,1,0:T(8,128)}, f32[2,256,128]{2,1,0:T(8,128)S(1)}, u32[]{:S(2)}) copy-start(f32[2,256,128]{2,1,0:T(8,128)S(1)} %multiply_subtract_fusion.9) | copy-start | bytes 786436
  610.1 7.0 collective-permute-start.24
  615.2 3.8 collective-permute-start.25
  619.2 11.1 %collective-permute-start.26 = (f32[2,384,64]{2,1,0:T(8,128)S(1)}, f32[2,384,64]{2,1,0:T(8,128)S(1)}, u32[]{:S(2)}, u32[]{:S(2)}) collective-permute-start(f32[2,384,64]{2,1,0:T(8,128)S(1)} %get-tuple-element.258), channel_id=1, source_target_pairs={{0,1},{1,2},{2,3},{3,4},{4,5},{5,6},{6,7},{8,9},{9,10},{10,11},{11... | collective-permute-start | bytes 589832 | tf_op jit(solution)/shard_map/ppermute | solution.py:28
  622.5 18.1 %collective-permute-start.27 = (f32[2,384,64]{2,1,0:T(8,128)S(1)}, f32[2,384,64]{2,1,0:T(8,128)S(1)}, u32[]{:S(2)}, u32[]{:S(2)}) collective-permute-start(f32[2,384,64]{2,1,0:T(8,128)S(1)} %get-tuple-element.259), channel_id=1, source_target_pairs={{1,0},{2,1},{3,2},{4,3},{5,4},{6,5},{7,6},{9,8},{10,9},{11,10},{12... | collective-permute-start | bytes 589832 | tf_op jit(solution)/shard_map/ppermute | solution.py:29
  651.8 2.7 copy-start.14
  677.2 327.8 %all-reduce.13.cloned.1.call-start = ((), (), s32[]{:S(2)}) async-start(), calls=%async_computation.2 | async-start | bytes 1572864 | tf_op jit(solution)/shard_map/psum | solution.py:17
  677.4 13.2 %collective-permute-start.28 = (f32[2,384,64]{2,1,0:T(8,128)S(1)}, f32[2,384,64]{2,1,0:T(8,128)S(1)}, u32[]{:S(2)}, u32[]{:S(2)}) collective-permute-start(f32[2,384,64]{2,1,0:T(8,128)S(1)} %get-tuple-element.245), channel_id=1, source_target_pairs={{0,1},{1,2},{2,3},{3,4},{4,5},{5,6},{6,7},{8,9},{9,10},{10,11},{11... | collective-permute-start | bytes 589832 | tf_op jit(solution)/shard_map/ppermute | solution.py:37
  682.4 22.6 %collective-permute-start.29 = (f32[2,384,64]{2,1,0:T(8,128)S(1)}, f32[2,384,64]{2,1,0:T(8,128)S(1)}, u32[]{:S(2)}, u32[]{:S(2)}) collective-permute-start(f32[2,384,64]{2,1,0:T(8,128)S(1)} %get-tuple-element.244), channel_id=1, source_target_pairs={{1,0},{2,1},{3,2},{4,3},{5,4},{6,5},{7,6},{9,8},{10,9},{11,10},{12... | collective-permute-start | bytes 589832 | tf_op jit(solution)/shard_map/ppermute | solution.py:37
  705.1 209.9 %copy-start.3 = (f32[2,256,128]{2,1,0:T(8,128)S(1)}, f32[2,256,128]{2,1,0:T(8,128)}, u32[]{:S(2)}) copy-start(f32[2,256,128]{2,1,0:T(8,128)} %copy-done.2) | copy-start | bytes 786436
  905.8 7.3 collective-permute-start.30
  907.9 7.1 collective-permute-start.31
Sparse Core Ops, SparseCore 0:
  220.5 223.5 all-reduce.10
  446.8 97.1 all-reduce.14
  677.3 228.3 all-reduce.8
  908.3 96.6 all-reduce.12
